TPU v7x, 32 devices: a whole 2x2x4 slice. The times are simulated.
32 devices in a mesh: row: 8 (over z, x), col: 4 (over y, core).
Axes of the slice: x: 2, y: 2, z: 4, core: 2. Of those that a mesh axis runs over, the one named last changes fastest.
Arguments:
- tokens: bfloat16 [64, 512, 512], P('row', 'col'), may hold values from -6 to 6
- ln1_gain: float32 [512], replicated, may hold values from 0.1 to 1.9
- w_qkv: bfloat16 [512, 1536], replicated
- rel_bias: float32 [16, 49], replicated, may hold values from -4 to 4
- w_proj: bfloat16 [512, 512], replicated, may hold values from -0.25 to 0.25
- ln2_gain: float32 [512], replicated, may hold values from 0.1 to 1.9
- w_up: bfloat16 [512, 2048], replicated, may hold values from -0.25 to 0.25
- w_down: bfloat16 [2048, 512], replicated, may hold values from -0.125 to 0.125
- merge_gain: float32 [2048], replicated, may hold values from 0.3 to 3
- w_merge: bfloat16 [2048, 1024], replicated, may hold values from -0.125 to 0.125
- cotangent: bfloat16 [32, 256, 1024], P('row', 'col'), may hold values from -6 to 6
Outputs:
- merged: bfloat16 [32, 256, 1024], P('row', 'col')
- grad_merge: float32 [2048, 1024], P(('row', 'col'))
- grad_down: float32 [2048, 512], P(('row', 'col'))
All inputs are finite; a program needn't handle non-finite values.
Results may differ from a plain program's by a relative error of at most 0.012.
Values may be sent and summed in bfloat16 or wider, within the bound.
A program may use at most 128 MiB of HBM per device.

v0:
```python
import jax
import jax.numpy as jnp
from jax import lax
from jax.sharding import PartitionSpec as P


def with_halo(cells, sides, width):
    for axis, dim in sides:
        count = lax.axis_size(axis)
        ends = count - 1
        head = lax.slice_in_dim(cells, 0, width, axis=dim)
        tail = lax.slice_in_dim(cells, cells.shape[dim] - width, cells.shape[dim], axis=dim)
        cells = jnp.concatenate(
            [
                lax.ppermute(tail, axis, [(i, (i + 1) % count) for i in range(ends)]),
                cells,
                lax.ppermute(head, axis, [((i + 1) % count, i) for i in range(ends)]),
            ],
            axis=dim,
        )
    return cells


def layer_norm(value, gain):
    mean = jnp.mean(value, axis=-1, keepdims=True)
    var = jnp.mean((value - mean) ** 2, axis=-1, keepdims=True)
    return (value - mean) / jnp.sqrt(var + 1e-05) * gain


def local(
    tokens,
    ln1_gain,
    w_qkv,
    rel_bias,
    w_proj,
    ln2_gain,
    w_up,
    w_down,
    merge_gain,
    w_merge,
    cotangent,
):
    rows, cols, width = tokens.shape
    heads = rel_bias.shape[0]
    head_dim = width // heads
    x_flat = tokens.astype(jnp.float32).reshape(-1, width)
    normed = layer_norm(x_flat, ln1_gain).astype(jnp.bfloat16)
    query = jnp.dot(normed, w_qkv[:, :width], preferred_element_type=jnp.float32).astype(
        jnp.bfloat16
    )
    query_t = query.reshape(rows, cols, heads, head_dim).transpose(0, 2, 3, 1)
    keyval = jnp.dot(normed, w_qkv[:, width:], preferred_element_type=jnp.float32).astype(
        jnp.bfloat16
    )
    keyval = keyval.reshape(rows, cols, 2 * width).transpose(0, 2, 1)
    padded = with_halo(keyval, (("row", 0), ("col", 2)), 3)
    padded = padded.reshape(rows + 6, 2, heads, head_dim, cols + 6)
    total_rows = rows * lax.axis_size("row")
    total_cols = cols * lax.axis_size("col")
    row_pos = lax.axis_index("row") * rows + jnp.arange(rows)
    col_pos = lax.axis_index("col") * cols + jnp.arange(cols)
    scores = []
    masks = []
    for di in range(7):
        for dj in range(7):
            key = padded[di : di + rows, 0, :, :, dj : dj + cols]
            scores.append(
                jnp.einsum("rhdc,rhdc->rhc", query_t, key, preferred_element_type=jnp.float32)
            )
            rows_ok = (row_pos + di - 3 >= 0) & (row_pos + di - 3 < total_rows)
            cols_ok = (col_pos + dj - 3 >= 0) & (col_pos + dj - 3 < total_cols)
            masks.append(rows_ok[:, None] & cols_ok[None, :])
    scale = 1.0 / jnp.sqrt(jnp.float32(head_dim))
    score = jnp.stack(scores, 0) * scale + rel_bias.T[:, None, :, None]
    valid = jnp.stack(masks, 0)[:, :, None, :]
    score = jnp.where(valid, score, -1e30)
    top = jnp.max(score, axis=0, keepdims=True)
    expo = jnp.where(valid, jnp.exp(score - top), 0.0)
    probs = (expo / jnp.sum(expo, axis=0, keepdims=True)).astype(jnp.bfloat16)
    attn = jnp.zeros((rows, heads, head_dim, cols), jnp.float32)
    offset = 0
    for di in range(7):
        for dj in range(7):
            value = padded[di : di + rows, 1, :, :, dj : dj + cols]
            attn = attn + jnp.einsum(
                "rhc,rhdc->rhdc", probs[offset], value, preferred_element_type=jnp.float32
            )
            offset += 1
    attn = attn.astype(jnp.bfloat16).transpose(0, 3, 1, 2).reshape(-1, width)
    h_one = (x_flat + jnp.dot(attn, w_proj, preferred_element_type=jnp.float32)).astype(
        jnp.bfloat16
    )
    normed2 = layer_norm(h_one.astype(jnp.float32), ln2_gain).astype(jnp.bfloat16)
    hidden = jax.nn.gelu(
        jnp.dot(normed2, w_up, preferred_element_type=jnp.float32), approximate=False
    ).astype(jnp.bfloat16)
    out_y = (
        h_one.astype(jnp.float32) + jnp.dot(hidden, w_down, preferred_element_type=jnp.float32)
    ).astype(jnp.bfloat16)
    joined = (
        out_y.reshape(rows // 2, 2, cols // 2, 2, width)
        .transpose(0, 2, 3, 1, 4)
        .reshape(-1, 4 * width)
        .astype(jnp.float32)
    )
    mean = jnp.mean(joined, axis=-1, keepdims=True)
    inv = 1.0 / jnp.sqrt(jnp.mean((joined - mean) ** 2, axis=-1, keepdims=True) + 1e-05)
    unit = (joined - mean) * inv
    merge_in = (unit * merge_gain).astype(jnp.bfloat16)
    merged = jnp.dot(merge_in, w_merge, preferred_element_type=jnp.float32).astype(jnp.bfloat16)
    merged = merged.reshape(rows // 2, cols // 2, 2 * width)
    cot = cotangent.reshape(-1, 2 * width)
    grad_m = jnp.dot(merge_in.T, cot, preferred_element_type=jnp.float32)
    grad_n = jnp.dot(cot, w_merge.T, preferred_element_type=jnp.float32) * merge_gain
    grad_z = (
        grad_n
        - jnp.mean(grad_n, axis=-1, keepdims=True)
        - unit * jnp.mean(grad_n * unit, axis=-1, keepdims=True)
    ) * inv
    grad_y = (
        grad_z.astype(jnp.bfloat16)
        .reshape(rows // 2, cols // 2, 2, 2, width)
        .transpose(0, 3, 1, 2, 4)
        .reshape(-1, width)
    )
    grad_d = jnp.dot(hidden.T, grad_y, preferred_element_type=jnp.float32)
    count = grad_m.size + grad_d.size
    sum_m, sum_d = lax.psum((grad_m, grad_d), ("row", "col"))
    total = jnp.sum(sum_m * sum_m) + jnp.sum(sum_d * sum_d)
    groups = lax.axis_size(("row", "col"))
    index = lax.axis_index(("row", "col"))
    share_m = lax.dynamic_slice_in_dim(
        sum_m, index * (sum_m.shape[0] // groups), sum_m.shape[0] // groups, 0
    )
    share_d = lax.dynamic_slice_in_dim(
        sum_d, index * (sum_d.shape[0] // groups), sum_d.shape[0] // groups, 0
    )
    factor = 1.0 / jnp.sqrt(total / count + 1e-06)
    return (merged, share_m * factor, share_d * factor)


def solution(mesh):
    placed = (
        P("row", "col", None),
        P(),
        P(),
        P(),
        P(),
        P(),
        P(),
        P(),
        P(),
        P(),
        P("row", "col", None),
    )
    return jax.shard_map(
        local,
        mesh=mesh,
        in_specs=placed,
        out_specs=(P("row", "col", None), P(("row", "col"), None), P(("row", "col"), None)),
        check_vma=False,
    )
```

profile of v0, /device:TPU:0, one launch (start us, length us, event | category | flops | bytes accessed | tf_op | source)
XLA Modules:
  0.0 520.8 jit_solution(10870981523958563618)
XLA Ops:
  13.7 3.9 copy.119
  20.2 5.8 %collective-permute-start = (bf16[3,1024,128]{2,1,0:T(8,128)(2,1)}, bf16[3,1024,128]{2,1,0:T(8,128)(2,1)}, u32[]{:S(2)}, u32[]{:S(2)}) collective-permute-start(bf16[3,1024,128]{2,1,0:T(8,128)(2,1)} %get-tuple-element.58), channel_id=1, source_target_pairs={{0,4},{4,8},{8,12},{12,16},{16,20},{20,24},{24,28},{1,5},{5,9},{9,... | collective-permute-start | bytes 2359304 | tf_op jit(solution)/shard_map/ppermute | solution.py:15
  39.6 19.4 %collective-permute-done = bf16[3,1024,128]{2,1,0:T(8,128)(2,1)} collective-permute-done((bf16[3,1024,128]{2,1,0:T(8,128)(2,1)}, bf16[3,1024,128]{2,1,0:T(8,128)(2,1)}, u32[]{:S(2)}, u32[]{:S(2)}) %collective-permute-start) | collective-permute-done | bytes 786464 | tf_op jit(solution)/shard_map/ppermute | solution.py:15
  60.6 4.3 fusion.140
  64.9 3.7 copy.120
  68.6 3.7 copy.121
  73.6 4.2 collective-permute-start.2
  78.6 3.9 copy.122
  82.4 3.1 copy.123
  85.6 8.4 %pad_maximum_fusion = bf16[14,1024,134]{2,1,0:T(8,128)(2,1)S(1)} fusion(bf16[14,1024,3]{2,1,0:T(8,128)(2,1)} %copy.123, bf16[3,1024,128]{2,1,0:T(8,128)(2,1)} %collective-permute-done.1, bf16[8,1024,128]{2,1,0:T(8,128)(2,1)} %bitcast.1631, bf16[3,1024,128]{2,1,0:T(8,128)(2,1)} %collective-permute-done, bf16[14,1024,3]{2,1,0:T(8,128)(2,1)} %copy.122), kind=kLoop, calls=%fused_computation.20 | loop fusion | flops 19210240 | bytes 7684096 | tf_op jit(solution)/shard_map/concatenate | solution.py:13
  94.0 7.9 %multiply_reduce_fusion.38 = (f32[8,16,128]{2,1,0:T(8,128)}, f32[8,16,128]{2,1,0:T(8,128)}, f32[8,16,128]{2,1,0:T(8,128)}, f32[8,16,128]{2,1,0:T(8,128)}, f32[8,...) fusion(bf16[14,2,16,32,134]{4,3,2,1,0:T(8,128)(2,1)S(1)} %bitca, ...), kind=kLoop, calls=%fused_computation.230 | loop fusion | flops 20234240 | bytes 16580608 | tf_op jit(solution)/shard_map/rhdc,rhdc->rhc/dot_general | solution.py:68
  101.9 12.3 %multiply_reduce_fusion.20 = (f32[8,16,128]{2,1,0:T(8,128)}, f32[8,16,128]{2,1,0:T(8,128)}, f32[8,16,128]{2,1,0:T(8,128)}, f32[8,16,128]{2,1,0:T(8,128)}, f32[8,...) fusion(bf16[14,2,16,32,134]{4,3,2,1,0:T(8,128)(2,1)S(1)} %bitca, ...), kind=kLoop, calls=%fused_computation.212 | loop fusion | flops 28016640 | bytes 22151168 | tf_op jit(solution)/shard_map/rhdc,rhdc->rhc/dot_general | solution.py:68
  114.2 11.7 %multiply_reduce_fusion.2 = (f32[8,16,128]{2,1,0:T(8,128)S(1)}, f32[8,16,128]{2,1,0:T(8,128)S(1)}, f32[8,16,128]{2,1,0:T(8,128)S(1)}, f32[8,16,128]{2,1,0:T(8,12...) fusion(bf16[14,2,16,32,134]{4,3,2,1,0:T(8,128)(2,1)S(1)} %bitca, ...), kind=kLoop, calls=%fused_computation.194 | loop fusion | flops 28016640 | bytes 22151168 | tf_op jit(solution)/shard_map/rhdc,rhdc->rhc/dot_general | solution.py:68
  146.3 43.1 %fusion.19 = bf16[8,128,16,32]{1,3,2,0:T(8,128)(2,1)} fusion(bf16[14,2,16,32,134]{4,3,2,1,0:T(8,128)(2,1)} %bitcast.1629, f32[8,128,16]{1,2,0:T(8,128)} %get-tuple-element.61, f32[8,128,16]{1,2,0:T(8,128)} %get-tuple-element.62, f32[8,128,16]{1,2,0:T(8,128)} %get-tuple-element.63, f32[8,128,16]{1,2,0:T(8,128)} %get-tuple-element.64, ...), kind=kLoop, calls=%fused_computation.40 | loop fusion | flops 77070336 | bytes 55640064 | tf_op jit(solution)/shard_map/convert_element_type | solution.py:89
  192.8 20.9 %fusion.2 = bf16[1024,2048]{1,0:T(8,128)(2,1)S(1)} fusion(bf16[512,2048]{1,0:T(8,128)(2,1)S(1)} %copy-done, bf16[1024,512]{1,0:T(8,128)(2,1)S(1)} %get-tuple-element.112, f32[512]{0:T(512)S(1)} %copy-done.35, f32[1024]{0:T(1024)S(1)} %add_sqrt_fusion, f32[1024]{0:T(1024)S(1)} %broadcast_multiply_fusion), kind=kOutput, calls=%fused_computation.3 | convolution fusion | flops 2286419968 | bytes 7350272 | tf_op jit(solution)/shard_map/dot_general | solution.py:95
  215.6 3.7 fusion.122
  223.6 4.2 multiply_reduce_fusion.52
  238.5 3.9 fusion.139
  252.4 6.8 %fusion.143 = f32[2048,512]{1,0:T(8,128)} fusion(bf16[1024,2048]{1,0:T(8,128)(2,1)} %copy-done.36, bf16[1024,512]{1,0:T(8,128)(2,1)} %reshape.2694), kind=kOutput, calls=%fused_computation.594 | convolution fusion | flops 2147483648 | bytes 9437184 | tf_op jit(solution)/shard_map/dot_general | solution.py:126
  259.2 4.5 fusion.142
  263.8 4.3 convolution_convert_fusion.2
  268.1 230.6 %all-reduce.3.cloned.1.call-done = (f32[2048,1024]{1,0:T(8,128)}, f32[2048,512]{1,0:T(8,128)}) async-done(((f32[2048,1024]{1,0:T(8,128)}, f32[2048,512]{1,0:T(8,128)}), (f32[2048,1024]{1,0:T(8,128)}, f32[2048,512]{1,0:T(8,128)})) %all-reduce.3.cloned.1.call-update) | async-done | bytes 12582928 | tf_op jit(solution)/shard_map/psum | solution.py:128
  498.6 3.9 multiply_reduce_fusion.1
  502.5 6.3 %multiply_reduce_fusion = f32[]{:T(128)} fusion(f32[2048,1024]{1,0:T(8,128)} %get-tuple-element.54), kind=kLoop, calls=%fused_computation.4 | loop fusion | flops 4194303 | bytes 8388612 | tf_op jit(solution)/shard_map/reduce_sum | solution.py:129
  (230 shorter events, 79.6 us)
Async XLA Ops:
  7.2 185.6 %copy-start = (bf16[512,2048]{1,0:T(8,128)(2,1)S(1)}, bf16[512,2048]{1,0:T(8,128)(2,1)}, u32[]{:S(2)}) copy-start(bf16[512,2048]{1,0:T(8,128)(2,1)} %param.17) | copy-start | bytes 6291460
  7.2 491.4 %all-reduce.3.cloned.1.call-start = ((), (), s32[]{:S(2)}) async-start(), calls=%async_computation | async-start | bytes 25165824 | tf_op jit(solution)/shard_map/psum | solution.py:128
  20.2 38.8 %collective-permute-start = (bf16[3,1024,128]{2,1,0:T(8,128)(2,1)}, bf16[3,1024,128]{2,1,0:T(8,128)(2,1)}, u32[]{:S(2)}, u32[]{:S(2)}) collective-permute-start(bf16[3,1024,128]{2,1,0:T(8,128)(2,1)} %get-tuple-element.58), channel_id=1, source_target_pairs={{0,4},{4,8},{8,12},{12,16},{16,20},{20,24},{24,28},{1,5},{5,9},{9,... | collective-permute-start | bytes 2359304 | tf_op jit(solution)/shard_map/ppermute | solution.py:15
  26.0 33.1 %collective-permute-start.1 = (bf16[3,1024,128]{2,1,0:T(8,128)(2,1)}, bf16[3,1024,128]{2,1,0:T(8,128)(2,1)}, u32[]{:S(2)}, u32[]{:S(2)}) collective-permute-start(bf16[3,1024,128]{2,1,0:T(8,128)(2,1)} %get-tuple-element.59), channel_id=1, source_target_pairs={{4,0},{8,4},{12,8},{16,12},{20,16},{24,20},{28,24},{5,1},{9,5},{13... | collective-permute-start | bytes 2359304 | tf_op jit(solution)/shard_map/ppermute | solution.py:17
  37.9 21.1 %copy-start.4 = (bf16[8,128,1024]{1,2,0:T(8,128)(2,1)S(1)}, bf16[8,128,1024]{1,2,0:T(8,128)(2,1)}, u32[]{:S(2)}) copy-start(bf16[8,128,1024]{1,2,0:T(8,128)(2,1)} %copy.119) | copy-start | bytes 6291460
  72.3 10.1 %collective-permute-start.3 = (bf16[14,1024,3]{1,0,2:T(8,128)(2,1)S(1)}, bf16[14,1024,3]{1,0,2:T(8,128)(2,1)S(1)}, u32[]{:S(2)}, u32[]{:S(2)}) collective-permute-start(bf16[14,1024,3]{1,0,2:T(8,128)(2,1)S(1)} %copy.121), channel_id=1, source_target_pairs={{1,0},{2,1},{3,2},{5,4},{6,5},{7,6},{9,8},{10,9},{11,10},{13,12},{... | collective-permute-start | bytes 258056 | tf_op jit(solution)/shard_map/ppermute | solution.py:17
  73.6 5.0 collective-permute-start.2
  94.0 20.2 %copy-start.2 = (bf16[14,1024,134]{2,1,0:T(8,128)(2,1)}, bf16[14,1024,134]{2,1,0:T(8,128)(2,1)S(1)}, u32[]{:S(2)}) copy-start(bf16[14,1024,134]{2,1,0:T(8,128)(2,1)S(1)} %pad_maximum_fusion) | copy-start | bytes 11526148
  125.9 13.9 %copy-start.24 = (f32[8,16,128]{2,1,0:T(8,128)S(1)}, f32[8,16,128]{2,1,0:T(8,128)}, u32[]{:S(2)}) copy-start(f32[8,16,128]{2,1,0:T(8,128)} %get-tuple-element.33) | copy-start | bytes 196612
  125.9 13.9 %copy-start.23 = (f32[8,16,128]{2,1,0:T(8,128)S(1)}, f32[8,16,128]{2,1,0:T(8,128)}, u32[]{:S(2)}) copy-start(f32[8,16,128]{2,1,0:T(8,128)} %get-tuple-element.32) | copy-start | bytes 196612
  125.9 14.0 %copy-start.22 = (f32[8,16,128]{2,1,0:T(8,128)S(1)}, f32[8,16,128]{2,1,0:T(8,128)}, u32[]{:S(2)}) copy-start(f32[8,16,128]{2,1,0:T(8,128)} %get-tuple-element.31) | copy-start | bytes 196612
  125.9 14.0 %copy-start.21 = (f32[8,16,128]{2,1,0:T(8,128)S(1)}, f32[8,16,128]{2,1,0:T(8,128)}, u32[]{:S(2)}) copy-start(f32[8,16,128]{2,1,0:T(8,128)} %get-tuple-element.30) | copy-start | bytes 196612
  125.9 14.0 %copy-start.20 = (f32[8,16,128]{2,1,0:T(8,128)S(1)}, f32[8,16,128]{2,1,0:T(8,128)}, u32[]{:S(2)}) copy-start(f32[8,16,128]{2,1,0:T(8,128)} %get-tuple-element.29) | copy-start | bytes 196612
  125.9 14.0 %copy-start.19 = (f32[8,16,128]{2,1,0:T(8,128)S(1)}, f32[8,16,128]{2,1,0:T(8,128)}, u32[]{:S(2)}) copy-start(f32[8,16,128]{2,1,0:T(8,128)} %get-tuple-element.28) | copy-start | bytes 196612
  125.9 14.0 %copy-start.18 = (f32[8,16,128]{2,1,0:T(8,128)S(1)}, f32[8,16,128]{2,1,0:T(8,128)}, u32[]{:S(2)}) copy-start(f32[8,16,128]{2,1,0:T(8,128)} %get-tuple-element.27) | copy-start | bytes 196612
  125.9 14.0 %copy-start.17 = (f32[8,16,128]{2,1,0:T(8,128)S(1)}, f32[8,16,128]{2,1,0:T(8,128)}, u32[]{:S(2)}) copy-start(f32[8,16,128]{2,1,0:T(8,128)} %get-tuple-element.26) | copy-start | bytes 196612
  126.0 14.0 %copy-start.16 = (f32[8,16,128]{2,1,0:T(8,128)S(1)}, f32[8,16,128]{2,1,0:T(8,128)}, u32[]{:S(2)}) copy-start(f32[8,16,128]{2,1,0:T(8,128)} %get-tuple-element.25) | copy-start | bytes 196612
  126.0 14.1 %copy-start.15 = (f32[8,16,128]{2,1,0:T(8,128)S(1)}, f32[8,16,128]{2,1,0:T(8,128)}, u32[]{:S(2)}) copy-start(f32[8,16,128]{2,1,0:T(8,128)} %get-tuple-element.24) | copy-start | bytes 196612
  126.0 14.1 %copy-start.14 = (f32[8,16,128]{2,1,0:T(8,128)S(1)}, f32[8,16,128]{2,1,0:T(8,128)}, u32[]{:S(2)}) copy-start(f32[8,16,128]{2,1,0:T(8,128)} %get-tuple-element.23) | copy-start | bytes 196612
  126.0 14.1 %copy-start.13 = (f32[8,16,128]{2,1,0:T(8,128)S(1)}, f32[8,16,128]{2,1,0:T(8,128)}, u32[]{:S(2)}) copy-start(f32[8,16,128]{2,1,0:T(8,128)} %get-tuple-element.22) | copy-start | bytes 196612
  126.0 14.1 %copy-start.12 = (f32[8,16,128]{2,1,0:T(8,128)S(1)}, f32[8,16,128]{2,1,0:T(8,128)}, u32[]{:S(2)}) copy-start(f32[8,16,128]{2,1,0:T(8,128)} %get-tuple-element.21) | copy-start | bytes 196612
  126.0 14.1 %copy-start.11 = (f32[8,16,128]{2,1,0:T(8,128)S(1)}, f32[8,16,128]{2,1,0:T(8,128)}, u32[]{:S(2)}) copy-start(f32[8,16,128]{2,1,0:T(8,128)} %get-tuple-element.20) | copy-start | bytes 196612
  126.0 14.1 %copy-start.10 = (f32[8,16,128]{2,1,0:T(8,128)S(1)}, f32[8,16,128]{2,1,0:T(8,128)}, u32[]{:S(2)}) copy-start(f32[8,16,128]{2,1,0:T(8,128)} %get-tuple-element.19) | copy-start | bytes 196612
  192.8 22.8 %copy-start.32 = (bf16[2048,512]{1,0:T(8,128)(2,1)S(1)}, bf16[2048,512]{1,0:T(8,128)(2,1)}, u32[]{:S(2)}) copy-start(bf16[2048,512]{1,0:T(8,128)(2,1)} %param.18) | copy-start | bytes 6291460
  (18 other events, 122.0 us)
Sparse Core Ops, SparseCore 0:
  263.9 234.7 all-reduce.2
where the time goes:
time: 528 us; the launch traced here: 521 us
  waiting for transfers between devices  250 us (47%)
  other arithmetic  124 us (23%)
  local copies, waits for them, and re-layouts  66.4 us (13%)
  matrix products  50.6 us (10%)
  between operations  16.9 us (3%)
  starting transfers between devices  12.5 us (2%)
    psum x1, waiting for transfers between devices, local(): sum_m, sum_d = lax.psum((grad_m, grad_d), ('row', 'col'))  231 us
    convert_element_type x1, other arithmetic, local(): attn = attn.astype(jnp.bfloat16).transpose(0, 3, 1, 2).reshape(-1, width)  43.1 us
    dot_general x3, other arithmetic, local(): jnp.einsum('rhdc,rhdc->rhc', query_t, key, preferred_element_type=jnp.flo...  31.9 us
    dot_general x1, matrix products, local(): jnp.dot(normed2, w_up, preferred_element_type=jnp.float32)  20.9 us
    ppermute x2, waiting for transfers between devices, with_halo(): lax.ppermute(tail, axis, [(i, (i + 1) % count) for i in range(ends)])  19.4 us
    unnamed x123, local copies, waits for them, and re-layouts  17.5 us
    slice x3, local copies, waits for them, and re-layouts, with_halo(): lax.slice_in_dim(cells, cells.shape[dim] - width, cells.shape[dim], axis=...  10.6 us
  transfers between devices with their start and end apart: 5, of which 2 were waited for; matrix products, arithmetic and copies ran while one was open for 4% of the time, Pallas kernels for 0%

commit v1 on v0

--- a/solution.py
+++ b/solution.py
@@ -125,16 +125,12 @@
     )
     grad_d = jnp.dot(hidden.T, grad_y, preferred_element_type=jnp.float32)
     count = grad_m.size + grad_d.size
-    sum_m, sum_d = lax.psum((grad_m, grad_d), ("row", "col"))
-    total = jnp.sum(sum_m * sum_m) + jnp.sum(sum_d * sum_d)
-    groups = lax.axis_size(("row", "col"))
-    index = lax.axis_index(("row", "col"))
-    share_m = lax.dynamic_slice_in_dim(
-        sum_m, index * (sum_m.shape[0] // groups), sum_m.shape[0] // groups, 0
+    both = jnp.concatenate([grad_m.astype(jnp.bfloat16), grad_d.astype(jnp.bfloat16)], axis=1)
+    share = lax.psum_scatter(both, ("row", "col"), scatter_dimension=0, tiled=True).astype(
+        jnp.float32
     )
-    share_d = lax.dynamic_slice_in_dim(
-        sum_d, index * (sum_d.shape[0] // groups), sum_d.shape[0] // groups, 0
-    )
+    total = lax.psum(jnp.sum(share * share), ("row", "col"))
+    share_m, share_d = share[:, : grad_m.shape[1]], share[:, grad_m.shape[1] :]
     factor = 1.0 / jnp.sqrt(total / count + 1e-06)
     return (merged, share_m * factor, share_d * factor)
 

time: 528 us -> 447 us (0.85)
  waiting for transfers between devices: 250 us -> 136 us
  blocking collectives: 0 us -> 40 us
  local copies, waits for them, and re-layouts: 66.4 us -> 76.2 us
  other arithmetic: 124 us -> 116 us
    psum x1 -> x0, waiting for transfers between devices: 231 us -> none  [local(): sum_m, sum_d = lax.psum((grad_m, grad_d), ('row', 'col'))]
    unnamed x1 -> x2, waiting for transfers between devices: 0.02 us -> 116 us
    psum x0 -> x1, blocking collectives: none -> 40 us  [local(): total = lax.psum(jnp.sum(share * share), ('row', 'col'))]
    unnamed x123 -> x133, local copies, waits for them, and re-layouts: 17.5 us -> 30.3 us
    reduce_sum x2 -> x1, other arithmetic: 10.2 us -> 0.81 us  [local(): total = lax.psum(jnp.sum(share * share), ('row', 'col'))]
  transfers between devices with their start and end apart: 5 -> 5, of which waited for: 2 -> 2; matrix products, arithmetic and copies ran while one was open for 4% -> 5% of each run, Pallas kernels for 0% -> 0%
where the time goes in v1:
time: 447 us; the launch traced here: 440 us
  waiting for transfers between devices  136 us (30%)
  other arithmetic  116 us (26%)
  local copies, waits for them, and re-layouts  76.2 us (17%)
  matrix products  45.8 us (10%)
  blocking collectives  40 us (9%)
  between operations  15.9 us (4%)
  starting transfers between devices  10.2 us (2%)
    unnamed x2, waiting for transfers between devices  116 us
    convert_element_type x1, other arithmetic, local(): attn = attn.astype(jnp.bfloat16).transpose(0, 3, 1, 2).reshape(-1, width)  43 us
    psum x1, blocking collectives, local(): total = lax.psum(jnp.sum(share * share), ('row', 'col'))  40 us
    dot_general x3, other arithmetic, local(): jnp.einsum('rhdc,rhdc->rhc', query_t, key, preferred_element_type=jnp.flo...  31.9 us
    unnamed x133, local copies, waits for them, and re-layouts  30.3 us
    dot_general x1, matrix products, local(): jnp.dot(normed2, w_up, preferred_element_type=jnp.float32)  20.9 us
    ppermute x2, waiting for transfers between devices, with_halo(): lax.ppermute(tail, axis, [(i, (i + 1) % count) for i in range(ends)])  19.7 us
    slice x3, local copies, waits for them, and re-layouts, with_halo(): lax.slice_in_dim(cells, cells.shape[dim] - width, cells.shape[dim], axis=...  10.7 us
  transfers between devices with their start and end apart: 5, of which 2 were waited for; matrix products, arithmetic and copies ran while one was open for 5% of the time, Pallas kernels for 0%

profile of v1, /device:TPU:0, one launch (start us, length us, event | category | flops | bytes accessed | tf_op | source)
XLA Modules:
  0.0 440.3 jit_solution(13548229452154812814)
XLA Ops:
  13.7 3.9 copy.123
  20.3 5.8 %collective-permute-start = (bf16[3,1024,128]{2,1,0:T(8,128)(2,1)}, bf16[3,1024,128]{2,1,0:T(8,128)(2,1)}, u32[]{:S(2)}, u32[]{:S(2)}) collective-permute-start(bf16[3,1024,128]{2,1,0:T(8,128)(2,1)} %get-tuple-element.65), channel_id=1, source_target_pairs={{0,4},{4,8},{8,12},{12,16},{16,20},{20,24},{24,28},{1,5},{5,9},{9,... | collective-permute-start | bytes 2359304 | tf_op jit(solution)/shard_map/ppermute | solution.py:15
  39.4 19.7 %collective-permute-done = bf16[3,1024,128]{2,1,0:T(8,128)(2,1)} collective-permute-done((bf16[3,1024,128]{2,1,0:T(8,128)(2,1)}, bf16[3,1024,128]{2,1,0:T(8,128)(2,1)}, u32[]{:S(2)}, u32[]{:S(2)}) %collective-permute-start) | collective-permute-done | bytes 786464 | tf_op jit(solution)/shard_map/ppermute | solution.py:15
  60.7 4.3 fusion.140
  65.0 3.7 copy.124
  70.0 3.7 copy.125
  76.3 3.1 copy.126
  79.5 3.8 copy.127
  83.3 8.4 %pad_maximum_fusion = bf16[14,1024,134]{2,1,0:T(8,128)(2,1)S(1)} fusion(bf16[14,1024,3]{2,1,0:T(8,128)(2,1)} %copy.127, bf16[3,1024,128]{2,1,0:T(8,128)(2,1)} %collective-permute-done.1, bf16[8,1024,128]{2,1,0:T(8,128)(2,1)} %bitcast.1632, bf16[3,1024,128]{2,1,0:T(8,128)(2,1)} %collective-permute-done, bf16[14,1024,3]{2,1,0:T(8,128)(2,1)} %copy.126), kind=kLoop, calls=%fused_computation.19 | loop fusion | flops 19210240 | bytes 7684096 | tf_op jit(solution)/shard_map/concatenate | solution.py:13
  91.7 7.9 %multiply_reduce_fusion.36 = (f32[8,16,128]{2,1,0:T(8,128)}, f32[8,16,128]{2,1,0:T(8,128)}, f32[8,16,128]{2,1,0:T(8,128)}, f32[8,16,128]{2,1,0:T(8,128)}, f32[8,...) fusion(bf16[14,2,16,32,134]{4,3,2,1,0:T(8,128)(2,1)S(1)} %bitca, ...), kind=kLoop, calls=%fused_computation.231 | loop fusion | flops 20234240 | bytes 16580608 | tf_op jit(solution)/shard_map/rhdc,rhdc->rhc/dot_general | solution.py:68
  99.6 12.3 %multiply_reduce_fusion.18 = (f32[8,16,128]{2,1,0:T(8,128)}, f32[8,16,128]{2,1,0:T(8,128)}, f32[8,16,128]{2,1,0:T(8,128)}, f32[8,16,128]{2,1,0:T(8,128)}, f32[8,...) fusion(bf16[14,2,16,32,134]{4,3,2,1,0:T(8,128)(2,1)S(1)} %bitca, ...), kind=kLoop, calls=%fused_computation.213 | loop fusion | flops 28016640 | bytes 22151168 | tf_op jit(solution)/shard_map/rhdc,rhdc->rhc/dot_general | solution.py:68
  111.9 11.7 %multiply_reduce_fusion = (f32[8,16,128]{2,1,0:T(8,128)S(1)}, f32[8,16,128]{2,1,0:T(8,128)S(1)}, f32[8,16,128]{2,1,0:T(8,128)S(1)}, f32[8,16,128]{2,1,0:T(8,128)...) fusion(bf16[14,2,16,32,134]{4,3,2,1,0:T(8,128)(2,1)S(1)} %bitca, ...), kind=kLoop, calls=%fused_computation.195 | loop fusion | flops 28016640 | bytes 22151168 | tf_op jit(solution)/shard_map/rhdc,rhdc->rhc/dot_general | solution.py:68
  144.0 43.0 %fusion.19 = bf16[8,128,16,32]{1,3,2,0:T(8,128)(2,1)} fusion(bf16[14,2,16,32,134]{4,3,2,1,0:T(8,128)(2,1)} %bitcast.1630, f32[8,128,16]{1,2,0:T(8,128)} %get-tuple-element.68, f32[8,128,16]{1,2,0:T(8,128)} %get-tuple-element.69, f32[8,128,16]{1,2,0:T(8,128)} %get-tuple-element.70, f32[8,128,16]{1,2,0:T(8,128)} %get-tuple-element.71, ...), kind=kLoop, calls=%fused_computation.41 | loop fusion | flops 77070336 | bytes 55640064 | tf_op jit(solution)/shard_map/convert_element_type | solution.py:89
  190.5 20.9 %fusion.2 = bf16[1024,2048]{1,0:T(8,128)(2,1)S(1)} fusion(bf16[512,2048]{1,0:T(8,128)(2,1)S(1)} %copy-done, bf16[1024,512]{1,0:T(8,128)(2,1)S(1)} %get-tuple-element.119, f32[512]{0:T(512)S(1)} %copy-done.38, f32[1024]{0:T(1024)S(1)} %add_sqrt_fusion, f32[1024]{0:T(1024)S(1)} %broadcast_multiply_fusion), kind=kOutput, calls=%fused_computation.3 | convolution fusion | flops 2286419968 | bytes 7350272 | tf_op jit(solution)/shard_map/dot_general | solution.py:95
  213.3 3.7 fusion.122
  224.2 4.4 multiply_reduce_fusion.50
  233.2 3.1 reshape.2695
  236.3 4.5 %convolution_convert_fusion = bf16[2048,1024]{0,1:T(8,128)(2,1)} fusion(bf16[256,2048]{1,0:T(8,128)(2,1)S(1)} %convert_element_type.96, bf16[256,1024]{1,0:T(8,128)(2,1)} %bitcast.1638), kind=kOutput, calls=%fused_computation.21 | convolution fusion | flops 1075838976 | bytes 5767168 | tf_op jit(solution)/shard_map/dot_general | solution.py:113
  249.4 4.7 %convolution_convert_fusion.1 = bf16[2048,512]{0,1:T(8,128)(2,1)S(1)} fusion(bf16[1024,2048]{1,0:T(8,128)(2,1)} %copy-done.39, bf16[1024,512]{1,0:T(8,128)(2,1)S(1)} %reshape.2694), kind=kOutput, calls=%fused_computation.29 | convolution fusion | flops 2148532224 | bytes 7340032 | tf_op jit(solution)/shard_map/dot_general | solution.py:126
  254.1 3.5 pad_maximum_fusion.1
  257.6 8.8 %copy.476 = bf16[2048,1536]{1,0:T(8,128)(2,1)} copy(bf16[2048,1536]{0,1:T(8,128)(2,1)} %pad_maximum_fusion.1) | data formatting | bytes 12582912
  266.4 4.3 convolution_convert_fusion.4
  270.7 116.0 %reduce-scatter.4.cloned.1.call-done = bf16[64,1536]{1,0:T(8,128)(2,1)} async-done(((bf16[2048,1536]{1,0:T(8,128)(2,1)}), bf16[64,1536]{1,0:T(8,128)(2,1)}) %reduce-scatter.4.cloned.1.call-update) | async-done | bytes 196624
  388.9 40.0 %psum.7 = f32[]{:T(128)} all-reduce(f32[]{:T(128)} %multiply_reduce_fusion.51), channel_id=1, replica_groups=mesh['row'=8,'col'=4] {'row','col'}, use_global_device_ids=true, to_apply=%region_12.13 | all-reduce | flops 1 | bytes 8 | tf_op jit(solution)/shard_map/psum | solution.py:132
  (242 shorter events, 79.2 us)
Async XLA Ops:
  7.2 183.3 %copy-start = (bf16[512,2048]{1,0:T(8,128)(2,1)S(1)}, bf16[512,2048]{1,0:T(8,128)(2,1)}, u32[]{:S(2)}) copy-start(bf16[512,2048]{1,0:T(8,128)(2,1)} %param.17) | copy-start | bytes 6291460
  7.2 379.6 %reduce-scatter.4.cloned.1.call-start = ((), (), s32[]{:S(2)}) async-start(), calls=%async_computation.1 | async-start | bytes 6488064
  20.3 38.8 %collective-permute-start = (bf16[3,1024,128]{2,1,0:T(8,128)(2,1)}, bf16[3,1024,128]{2,1,0:T(8,128)(2,1)}, u32[]{:S(2)}, u32[]{:S(2)}) collective-permute-start(bf16[3,1024,128]{2,1,0:T(8,128)(2,1)} %get-tuple-element.65), channel_id=1, source_target_pairs={{0,4},{4,8},{8,12},{12,16},{16,20},{20,24},{24,28},{1,5},{5,9},{9,... | collective-permute-start | bytes 2359304 | tf_op jit(solution)/shard_map/ppermute | solution.py:15
  26.0 33.1 %collective-permute-start.1 = (bf16[3,1024,128]{2,1,0:T(8,128)(2,1)}, bf16[3,1024,128]{2,1,0:T(8,128)(2,1)}, u32[]{:S(2)}, u32[]{:S(2)}) collective-permute-start(bf16[3,1024,128]{2,1,0:T(8,128)(2,1)} %get-tuple-element.66), channel_id=1, source_target_pairs={{4,0},{8,4},{12,8},{16,12},{20,16},{24,20},{28,24},{5,1},{9,5},{13... | collective-permute-start | bytes 2359304 | tf_op jit(solution)/shard_map/ppermute | solution.py:17
  37.6 21.5 %copy-start.4 = (bf16[8,128,1024]{1,2,0:T(8,128)(2,1)S(1)}, bf16[8,128,1024]{1,2,0:T(8,128)(2,1)}, u32[]{:S(2)}) copy-start(bf16[8,128,1024]{1,2,0:T(8,128)(2,1)} %copy.123) | copy-start | bytes 6291460
  68.7 7.6 %collective-permute-start.2 = (bf16[14,1024,3]{1,0,2:T(8,128)(2,1)S(1)}, bf16[14,1024,3]{1,0,2:T(8,128)(2,1)S(1)}, u32[]{:S(2)}, u32[]{:S(2)}) collective-permute-start(bf16[14,1024,3]{1,0,2:T(8,128)(2,1)S(1)} %copy.124), channel_id=1, source_target_pairs={{0,1},{1,2},{2,3},{4,5},{5,6},{6,7},{8,9},{9,10},{10,11},{12,13},{... | collective-permute-start | bytes 258056 | tf_op jit(solution)/shard_map/ppermute | solution.py:15
  73.7 5.7 %collective-permute-start.3 = (bf16[14,1024,3]{1,0,2:T(8,128)(2,1)S(1)}, bf16[14,1024,3]{1,0,2:T(8,128)(2,1)}, u32[]{:S(2)}, u32[]{:S(2)}) collective-permute-start(bf16[14,1024,3]{1,0,2:T(8,128)(2,1)S(1)} %copy.125), channel_id=1, source_target_pairs={{1,0},{2,1},{3,2},{5,4},{6,5},{7,6},{9,8},{10,9},{11,10},{13,12},{... | collective-permute-start | bytes 258056 | tf_op jit(solution)/shard_map/ppermute | solution.py:17
  91.7 20.2 %copy-start.2 = (bf16[14,1024,134]{2,1,0:T(8,128)(2,1)}, bf16[14,1024,134]{2,1,0:T(8,128)(2,1)S(1)}, u32[]{:S(2)}) copy-start(bf16[14,1024,134]{2,1,0:T(8,128)(2,1)S(1)} %pad_maximum_fusion) | copy-start | bytes 11526148
  123.6 13.9 %copy-start.26 = (f32[8,16,128]{2,1,0:T(8,128)S(1)}, f32[8,16,128]{2,1,0:T(8,128)}, u32[]{:S(2)}) copy-start(f32[8,16,128]{2,1,0:T(8,128)} %get-tuple-element.41) | copy-start | bytes 196612
  123.6 14.0 %copy-start.25 = (f32[8,16,128]{2,1,0:T(8,128)S(1)}, f32[8,16,128]{2,1,0:T(8,128)}, u32[]{:S(2)}) copy-start(f32[8,16,128]{2,1,0:T(8,128)} %get-tuple-element.40) | copy-start | bytes 196612
  123.7 14.0 %copy-start.24 = (f32[8,16,128]{2,1,0:T(8,128)S(1)}, f32[8,16,128]{2,1,0:T(8,128)}, u32[]{:S(2)}) copy-start(f32[8,16,128]{2,1,0:T(8,128)} %get-tuple-element.39) | copy-start | bytes 196612
  123.7 14.0 %copy-start.23 = (f32[8,16,128]{2,1,0:T(8,128)S(1)}, f32[8,16,128]{2,1,0:T(8,128)}, u32[]{:S(2)}) copy-start(f32[8,16,128]{2,1,0:T(8,128)} %get-tuple-element.38) | copy-start | bytes 196612
  123.7 14.0 %copy-start.22 = (f32[8,16,128]{2,1,0:T(8,128)S(1)}, f32[8,16,128]{2,1,0:T(8,128)}, u32[]{:S(2)}) copy-start(f32[8,16,128]{2,1,0:T(8,128)} %get-tuple-element.37) | copy-start | bytes 196612
  123.7 14.0 %copy-start.21 = (f32[8,16,128]{2,1,0:T(8,128)S(1)}, f32[8,16,128]{2,1,0:T(8,128)}, u32[]{:S(2)}) copy-start(f32[8,16,128]{2,1,0:T(8,128)} %get-tuple-element.36) | copy-start | bytes 196612
  123.7 14.0 %copy-start.20 = (f32[8,16,128]{2,1,0:T(8,128)S(1)}, f32[8,16,128]{2,1,0:T(8,128)}, u32[]{:S(2)}) copy-start(f32[8,16,128]{2,1,0:T(8,128)} %get-tuple-element.35) | copy-start | bytes 196612
  123.7 14.0 %copy-start.19 = (f32[8,16,128]{2,1,0:T(8,128)S(1)}, f32[8,16,128]{2,1,0:T(8,128)}, u32[]{:S(2)}) copy-start(f32[8,16,128]{2,1,0:T(8,128)} %get-tuple-element.34) | copy-start | bytes 196612
  123.7 14.1 %copy-start.18 = (f32[8,16,128]{2,1,0:T(8,128)S(1)}, f32[8,16,128]{2,1,0:T(8,128)}, u32[]{:S(2)}) copy-start(f32[8,16,128]{2,1,0:T(8,128)} %get-tuple-element.33) | copy-start | bytes 196612
  123.7 14.1 %copy-start.17 = (f32[8,16,128]{2,1,0:T(8,128)S(1)}, f32[8,16,128]{2,1,0:T(8,128)}, u32[]{:S(2)}) copy-start(f32[8,16,128]{2,1,0:T(8,128)} %get-tuple-element.32) | copy-start | bytes 196612
  123.7 14.1 %copy-start.16 = (f32[8,16,128]{2,1,0:T(8,128)S(1)}, f32[8,16,128]{2,1,0:T(8,128)}, u32[]{:S(2)}) copy-start(f32[8,16,128]{2,1,0:T(8,128)} %get-tuple-element.31) | copy-start | bytes 196612
  123.7 14.1 %copy-start.15 = (f32[8,16,128]{2,1,0:T(8,128)S(1)}, f32[8,16,128]{2,1,0:T(8,128)}, u32[]{:S(2)}) copy-start(f32[8,16,128]{2,1,0:T(8,128)} %get-tuple-element.30) | copy-start | bytes 196612
  123.8 14.1 %copy-start.14 = (f32[8,16,128]{2,1,0:T(8,128)S(1)}, f32[8,16,128]{2,1,0:T(8,128)}, u32[]{:S(2)}) copy-start(f32[8,16,128]{2,1,0:T(8,128)} %get-tuple-element.29) | copy-start | bytes 196612
  123.8 14.1 %copy-start.13 = (f32[8,16,128]{2,1,0:T(8,128)S(1)}, f32[8,16,128]{2,1,0:T(8,128)}, u32[]{:S(2)}) copy-start(f32[8,16,128]{2,1,0:T(8,128)} %get-tuple-element.28) | copy-start | bytes 196612
  190.4 22.8 %copy-start.35 = (bf16[2048,512]{1,0:T(8,128)(2,1)S(1)}, bf16[2048,512]{1,0:T(8,128)(2,1)}, u32[]{:S(2)}) copy-start(bf16[2048,512]{1,0:T(8,128)(2,1)} %param.18) | copy-start | bytes 6291460
  386.8 46.5 %copy-start.1 = (bf16[512,2048]{1,0:T(8,128)(2,1)S(1)}, bf16[512,2048]{1,0:T(8,128)(2,1)}, u32[]{:S(2)}) copy-start(bf16[512,2048]{1,0:T(8,128)(2,1)} %param.17) | copy-start | bytes 6291460
  (21 other events, 140.5 us)
Sparse Core Ops, SparseCore 0:
  266.6 120.1 reduce-scatter.3

commit v2 on v1

v2 whole, which is shorter than its diff:
```python
import functools

import jax
import jax.numpy as jnp
from jax import lax
from jax.experimental import pallas as pl
from jax.experimental.pallas import tpu as pltpu
from jax.sharding import PartitionSpec as P

F32 = jnp.float32
BF16 = jnp.bfloat16
REACH = 3
SPAN = 2 * REACH + 1
TILE = 8
LEAD = 4
LOW = -1e30


def shifted(cells, axis, dim, width):
    count = lax.axis_size(axis)
    ends = count - 1
    size = cells.shape[dim]
    head = lax.slice_in_dim(cells, 0, width, axis=dim)
    tail = lax.slice_in_dim(cells, size - width, size, axis=dim)
    before = lax.ppermute(tail, axis, [(i, (i + 1) % count) for i in range(ends)])
    after = lax.ppermute(head, axis, [((i + 1) % count, i) for i in range(ends)])
    return before, after


def cost(flops, *arrays):
    return pl.CostEstimate(
        flops=flops,
        bytes_accessed=sum(a.size * a.dtype.itemsize for a in arrays),
        transcendentals=0,
    )


def normalise(value):
    mean = jnp.mean(value, axis=-1, keepdims=True)
    value = value - mean
    inv = 1.0 / jnp.sqrt(jnp.mean(value * value, axis=-1, keepdims=True) + 1e-05)
    return value * inv, inv


def dot(a, b, dims=((1,), (0,))):
    return lax.dot_general(a, b, (dims, ((), ())), preferred_element_type=F32)


def query_kernel(x_ref, gain_ref, w_ref, out_ref):
    unit, _ = normalise(x_ref[...].astype(F32))
    out_ref[...] = dot((unit * gain_ref[...]).astype(BF16), w_ref[...]).astype(BF16)


def back_kernel(cot_ref, w_ref, gain_ref, out_ref):
    out_ref[...] = dot(cot_ref[...], w_ref[...], ((1,), (1,))) * gain_ref[...]


def attend_kernel(
    heads, head_dim, x_ref, gain_ref, w_ref, q_ref, tab_ref, edge_ref, out_ref, kv_ref
):
    step = pl.program_id(0)
    width = gain_ref.shape[1]
    rows, span, _ = x_ref.shape
    block = rows * span
    unit, _ = normalise(x_ref[...].astype(F32).reshape(block, width))
    fresh = dot((unit * gain_ref[...]).astype(BF16), w_ref[...]).astype(BF16)
    kv_ref[:block, :] = kv_ref[block:, :]
    kv_ref[block:, :] = fresh

    @pl.when(step > 0)
    def _():
        groups = tab_ref.shape[0]
        each = width // groups
        per = heads // groups
        count = q_ref.shape[0]
        lane = lax.broadcasted_iota(jnp.int32, (1, each), 1)
        for g in range(groups):
            q = q_ref[:, g * each : (g + 1) * each]
            stacked = jnp.concatenate(
                [
                    jnp.where((lane >= h * head_dim) & (lane < (h + 1) * head_dim), q, jnp.zeros_like(q))
                    for h in range(per)
                ],
                axis=0,
            )
            key = kv_ref[:, g * each : (g + 1) * each]
            value = kv_ref[:, width + g * each : width + (g + 1) * each]
            score = dot(stacked, key, ((1,), (1,))) * (head_dim**-0.5)
            score = score + tab_ref[g] + edge_ref[0]
            top = jnp.max(score, axis=-1, keepdims=True)
            expo = jnp.exp(score - top)
            total = jnp.sum(expo, axis=-1, keepdims=True)
            probs = (expo * (1.0 / total)).astype(BF16)
            mixed = dot(probs, value)
            acc = jnp.zeros((count, each), F32)
            for h in range(per):
                part = mixed[h * count : (h + 1) * count]
                acc = jnp.where((lane >= h * head_dim) & (lane < (h + 1) * head_dim), part, acc)
            out_ref[:, g * each : (g + 1) * each] = acc.astype(BF16)


def mlp_kernel(
    sub, a_ref, x_ref, gain_ref, wp_ref, wu_ref, wd_ref, hid_ref, z_ref
):
    width = x_ref.shape[1]
    h_one = (x_ref[...].astype(F32) + dot(a_ref[...], wp_ref[...])).astype(BF16)
    unit, _ = normalise(h_one.astype(F32))
    normed = (unit * gain_ref[...]).astype(BF16)
    y = h_one.astype(F32)
    piece = 512
    for c in range(0, wu_ref.shape[1], piece):
        up = dot(normed, wu_ref[:, c : c + piece])
        hid = (0.5 * up * (1.0 + lax.erf(up * (0.5**0.5)))).astype(BF16)
        hid_ref[:, c : c + piece] = hid
        y = y + dot(hid, wd_ref[c : c + piece, :])
    y = y.astype(BF16)
    tiles = y.shape[0] // (4 * sub)
    for t in range(tiles):
        for p in range(4):
            at = (4 * t + p) * sub
            z_ref[t * sub : (t + 1) * sub, p * width : (p + 1) * width] = y[at : at + sub]


def grad_kernel(
    sub, z_ref, hid_ref, gn_ref, cot_ref, gain_ref, wm_ref, merged_ref, grad_ref, m_ref, dy_ref
):
    merged_tokens, wide = z_ref.shape
    width = wide // 4
    out_w = cot_ref.shape[1]
    chunk = 4 * sub

    @pl.loop(0, merged_tokens // chunk)
    def _(c):
        at = pl.ds(pl.multiple_of(c * chunk, chunk), chunk)
        unit, inv = normalise(z_ref[at, :].astype(F32))
        m_ref[at, :] = (unit * gain_ref[...]).astype(BF16)
        gn = gn_ref[at, :]
        gn = gn - jnp.mean(gn, axis=-1, keepdims=True) - unit * jnp.mean(
            gn * unit, axis=-1, keepdims=True
        )
        dz = (gn * inv).astype(BF16)
        for t in range(chunk // sub):
            for p in range(4):
                to = pl.multiple_of(c * (4 * chunk), 4 * chunk) + (4 * t + p) * sub
                dy_ref[pl.ds(to, sub), :] = dz[
                    t * sub : (t + 1) * sub, p * width : (p + 1) * width
                ]

    piece = 256

    @pl.loop(0, out_w // piece)
    def _(c):
        at = pl.ds(pl.multiple_of(c * piece, piece), piece)
        merged_ref[:, at] = dot(m_ref[...], wm_ref[:, at]).astype(BF16)

    @pl.loop(0, wide // piece)
    def _(c):
        at = pl.ds(pl.multiple_of(c * piece, piece), piece)
        grad_m = dot(m_ref[:, at], cot_ref[...], ((0,), (0,))).astype(BF16)
        for p in range(out_w // width):
            grad_ref[p, at, :] = grad_m[:, p * width : (p + 1) * width]
        grad_ref[out_w // width, at, :] = dot(
            hid_ref[:, at], dy_ref[...], ((0,), (0,))
        ).astype(BF16)


def place(dims, at, value):
    return tuple(value if d == at else slice(None) for d in dims)


def reduce_kernel(bits, orders, size, in_ref, om_ref, od_ref, *scratch):
    steps, parts = len(bits), len(orders)
    recv, scratch = scratch[:steps], scratch[steps:]
    work, scratch = scratch[: steps - 1], scratch[steps - 1 :]
    acc, v_send, v_recv, send_sem, recv_sem, vs_sem, vr_sem = scratch
    mine, peer = {}, {}
    for axis, weight in bits:
        here = lax.axis_index(axis)
        bit = (here // weight) % 2
        mine[axis, weight] = bit
        peer[axis, weight] = {axis: here + weight * (1 - 2 * bit)}

    barrier = pltpu.get_barrier_semaphore()
    for bit in bits:
        pl.semaphore_signal(
            barrier, inc=1, device_id=peer[bit], device_id_type=pl.DeviceIdType.MESH
        )
    pl.semaphore_wait(barrier, steps)

    def held(k, p):
        return [b for b in bits if b not in orders[p][:k]]

    def exchange(k, p):
        bit = orders[p][k]
        source = in_ref if k == 0 else work[k - 1]
        return pltpu.make_async_remote_copy(
            src_ref=source.at[(p,) + place(held(k, p), bit, 1 - mine[bit])],
            dst_ref=recv[k].at[p],
            send_sem=send_sem.at[k, p],
            recv_sem=recv_sem.at[k, p],
            device_id=peer[bit],
            device_id_type=pl.DeviceIdType.MESH,
        )

    flying = [exchange(0, p) for p in range(parts)]
    for copy in flying:
        copy.start()
    for k in range(steps):
        for p in range(parts):
            flying[p].wait()
            bit = orders[p][k]
            source = in_ref if k == 0 else work[k - 1]
            dims = held(k, p)
            left = [d for d in dims if d != bit]

            @pl.loop(0, 2 ** len(left))
            def _(j):
                digits = [(j // 2 ** (len(left) - 1 - n)) % 2 for n in range(len(left))]
                chosen = dict(zip(left, digits))
                own = tuple(mine[bit] if d == bit else chosen[d] for d in dims)
                value = source[(p,) + own].astype(F32) + recv[k][(p,) + tuple(digits)].astype(F32)
                if k < steps - 1:
                    work[k][(p,) + tuple(digits)] = value.astype(BF16)
                else:
                    acc[p] = value

            if k < steps - 1:
                flying[p] = exchange(k + 1, p)
                flying[p].start()

    total = jnp.zeros(v_send.shape[1:], F32)
    for p in range(parts):
        square = acc[p] * acc[p]
        for r in range(0, square.shape[0], 8):
            for c in range(0, square.shape[1], 128):
                total = total + square[r : r + 8, c : c + 128]
    for k, bit in enumerate(bits):
        v_send[k] = total
        copy = pltpu.make_async_remote_copy(
            src_ref=v_send.at[k],
            dst_ref=v_recv.at[k],
            send_sem=vs_sem.at[k],
            recv_sem=vr_sem.at[k],
            device_id=peer[bit],
            device_id_type=pl.DeviceIdType.MESH,
        )
        copy.start()
        copy.wait()
        total = total + v_recv[k]
    total = jnp.sum(jnp.sum(total, axis=0, keepdims=True), axis=1, keepdims=True)
    factor = 1.0 / jnp.sqrt(total / size + 1e-06)
    wide = od_ref.shape[1]
    for p in range(parts - 1):
        om_ref[:, p * wide : (p + 1) * wide] = acc[p] * factor
    od_ref[...] = acc[parts - 1] * factor


def reduce_grads(both):
    parts, tall, wide = both.shape
    bits = []
    for axis in ("row", "col"):
        weight = lax.axis_size(axis) // 2
        while weight:
            bits.append((axis, weight))
            weight //= 2
    steps = len(bits)
    first = [b for b in bits if b == ("col", 1)]
    swap = [b for b in (("row", 1), ("col", 2), ("row", 2)) if b in bits]
    rest = [b for b in bits[::-1] if b not in first and b not in swap]
    orders = []
    for p in range(parts):
        turn = p % max(1, len(swap))
        orders.append(tuple(first + swap[turn:] + swap[:turn] + rest))
    rows = tall // 2**steps
    shapes = [(parts,) + (2,) * (steps - 1 - k) + (rows, wide) for k in range(steps)]
    vector = pltpu.VMEM((steps, 8, 128), F32)
    return pl.pallas_call(
        functools.partial(reduce_kernel, tuple(bits), tuple(orders), both.size),
        in_specs=[pl.BlockSpec(memory_space=pltpu.VMEM)],
        out_specs=[pl.BlockSpec(memory_space=pltpu.VMEM)] * 2,
        out_shape=[
            jax.ShapeDtypeStruct((rows, (parts - 1) * wide), F32),
            jax.ShapeDtypeStruct((rows, wide), F32),
        ],
        scratch_shapes=[pltpu.VMEM(s, BF16) for s in shapes]
        + [pltpu.VMEM(s, BF16) for s in shapes[:-1]]
        + [
            pltpu.VMEM((parts, rows, wide), F32),
            vector,
            vector,
            pltpu.SemaphoreType.DMA((steps, parts)),
            pltpu.SemaphoreType.DMA((steps, parts)),
            pltpu.SemaphoreType.DMA((steps,)),
            pltpu.SemaphoreType.DMA((steps,)),
        ],
        compiler_params=pltpu.CompilerParams(
            collective_id=0, has_side_effects=True, vmem_limit_bytes=56 * 2**20
        ),
        name="reduce",
    )(both.reshape((parts,) + (2,) * steps + (rows, wide)))


def local(
    tokens,
    ln1_gain,
    w_qkv,
    rel_bias,
    w_proj,
    ln2_gain,
    w_up,
    w_down,
    merge_gain,
    w_merge,
    cotangent,
):
    rows, cols, width = tokens.shape
    heads = rel_bias.shape[0]
    head_dim = width // heads
    ff = w_up.shape[1]
    tiles = cols // TILE
    blocks = tiles + 1
    held = rows * TILE
    sub = held // 4
    near = (rows + 2 * REACH) * TILE
    count = rows * cols
    merged_count = count // 4
    params = pltpu.CompilerParams(vmem_limit_bytes=56 * 2**20)

    above, below = shifted(tokens, "row", 0, REACH)
    mine = (
        tokens.reshape(rows // 2, 2, tiles, TILE // 2, 2, width)
        .transpose(2, 4, 1, 0, 3, 5)
        .reshape(count, width)
    )
    cot = (
        cotangent.reshape(rows // 2, tiles, TILE // 2, 2 * width)
        .transpose(1, 0, 2, 3)
        .reshape(merged_count, 2 * width)
    )
    gain1 = ln1_gain[None, :]
    gain2 = ln2_gain[None, :]
    gain_m = merge_gain[None, :]

    step = count // 4
    query = pl.pallas_call(
        query_kernel,
        grid=(4,),
        in_specs=[
            pl.BlockSpec((step, width), lambda i: (i, 0)),
            pl.BlockSpec((1, width), lambda i: (0, 0)),
            pl.BlockSpec((width, width), lambda i: (0, 0)),
        ],
        out_specs=pl.BlockSpec((step, width), lambda i: (i, 0)),
        out_shape=jax.ShapeDtypeStruct((count, width), BF16),
        cost_estimate=cost(2 * count * width * width, mine, mine),
        name="query",
    )(mine, gain1, w_qkv)
    back = pl.pallas_call(
        back_kernel,
        grid=(4,),
        in_specs=[
            pl.BlockSpec((merged_count, 2 * width), lambda i: (0, 0)),
            pl.BlockSpec((width, 2 * width), lambda i: (i, 0)),
            pl.BlockSpec((1, width), lambda i: (0, i)),
        ],
        out_specs=pl.BlockSpec((merged_count, width), lambda i: (0, i)),
        out_shape=jax.ShapeDtypeStruct((merged_count, 4 * width), F32),
        cost_estimate=cost(16 * merged_count * width * width, cot, w_merge),
        name="back",
    )(cot, w_merge, gain_m)

    q_at = jnp.arange(held)
    q_col = q_at % (TILE // 2) * 2 + q_at // (2 * sub)
    q_row = q_at % sub // (TILE // 2) * 2 + q_at // sub % 2
    k_at = jnp.arange(2 * near)
    k_row = k_at % near // TILE
    k_col = k_at // near * TILE + k_at % TILE
    d_row = k_row[None, :] - q_row[:, None]
    d_col = k_col[None, :] - q_col[:, None] + (REACH - LEAD)
    inside = (d_row >= 0) & (d_row < SPAN) & (d_col >= 0) & (d_col < SPAN)
    where = jnp.where(inside, d_row * SPAN + d_col, -1)
    hot = (where[None] == jnp.arange(SPAN * SPAN)[:, None, None]).astype(F32)
    table = jnp.einsum("ho,oqk->hqk", rel_bias, hot, precision=lax.Precision.HIGHEST)
    groups = max(1, width // 256)
    table = jnp.where(inside, table, LOW).reshape(groups, heads // groups * held, 2 * near)
    total_rows = rows * lax.axis_size("row")
    total_cols = cols * lax.axis_size("col")
    at_row = lax.axis_index("row") * rows + k_row - REACH
    at_col = (
        lax.axis_index("col") * cols + (k_col - LEAD)[None, :] + TILE * jnp.arange(tiles)[:, None]
    )
    on_grid = (at_row >= 0) & (at_row < total_rows) & (at_col >= 0) & (at_col < total_cols)
    edge = jnp.where(on_grid, 0.0, LOW).astype(F32)[:, None, :]

    tall = jnp.concatenate([above, tokens, below], axis=0)
    left, right = shifted(tall, "col", 1, LEAD)
    padded = jnp.concatenate([left, tall, right], axis=1)

    last = lambda i: (jnp.maximum(i - 1, 0), 0)
    fixed2 = lambda i: (0, 0)
    attn = pl.pallas_call(
        functools.partial(attend_kernel, heads, head_dim),
        grid=(blocks,),
        in_specs=[
            pl.BlockSpec((rows + 2 * REACH, TILE, width), lambda i: (0, i, 0)),
            pl.BlockSpec((1, width), fixed2),
            pl.BlockSpec((width, 2 * width), fixed2),
            pl.BlockSpec((held, width), last),
            pl.BlockSpec(table.shape, lambda i: (0, 0, 0)),
            pl.BlockSpec((1, 1, 2 * near), lambda i: (jnp.maximum(i - 1, 0), 0, 0)),
        ],
        out_specs=pl.BlockSpec((held, width), last),
        out_shape=jax.ShapeDtypeStruct((count, width), BF16),
        scratch_shapes=[pltpu.VMEM((2 * near, 2 * width), BF16)],
        compiler_params=params,
        cost_estimate=cost(8 * count * 2 * width * width, padded, table),
        name="attend",
    )(padded, gain1, w_qkv[:, width:], query, table, edge)

    hidden, z = pl.pallas_call(
        functools.partial(mlp_kernel, sub),
        grid=(4,),
        in_specs=[
            pl.BlockSpec((step, width), lambda i: (i, 0)),
            pl.BlockSpec((step, width), lambda i: (i, 0)),
            pl.BlockSpec((1, width), fixed2),
            pl.BlockSpec((width, width), fixed2),
            pl.BlockSpec((width, ff), fixed2),
            pl.BlockSpec((ff, width), fixed2),
        ],
        out_specs=[
            pl.BlockSpec((step, ff), lambda i: (i, 0)),
            pl.BlockSpec((step // 4, 4 * width), lambda i: (i, 0)),
        ],
        out_shape=[
            jax.ShapeDtypeStruct((count, ff), BF16),
            jax.ShapeDtypeStruct((merged_count, 4 * width), BF16),
        ],
        compiler_params=params,
        cost_estimate=cost(4 * count * ff * width, w_up, w_down),
        name="mlp",
    )(attn, mine, gain2, w_proj, w_up, w_down)

    merged, both = pl.pallas_call(
        functools.partial(grad_kernel, sub),
        in_specs=[pl.BlockSpec(memory_space=pltpu.VMEM)] * 6,
        out_specs=[pl.BlockSpec(memory_space=pltpu.VMEM)] * 2,
        out_shape=[
            jax.ShapeDtypeStruct((merged_count, 2 * width), BF16),
            jax.ShapeDtypeStruct((3, 4 * width, width), BF16),
        ],
        scratch_shapes=[
            pltpu.VMEM((merged_count, 4 * width), BF16),
            pltpu.VMEM((count, width), BF16),
        ],
        compiler_params=params,
        cost_estimate=cost(2 * count * ff * width, hidden),
        name="grads",
    )(z, hidden, back, cot, gain_m, w_merge)

    merged = (
        merged.reshape(tiles, rows // 2, TILE // 2, 2 * width)
        .transpose(1, 0, 2, 3)
        .reshape(rows // 2, cols // 2, 2 * width)
    )
    grad_merge, grad_down = reduce_grads(both)
    return (merged, grad_merge, grad_down)


def solution(mesh):
    placed = (
        P("row", "col", None),
        P(),
        P(),
        P(),
        P(),
        P(),
        P(),
        P(),
        P(),
        P(),
        P("row", "col", None),
    )
    return jax.shard_map(
        local,
        mesh=mesh,
        in_specs=placed,
        out_specs=(P("row", "col", None), P(("row", "col"), None), P(("row", "col"), None)),
        check_vma=False,
    )
```

time: 447 us -> 173 us (0.39); the launches traced: 440 us -> 172 us
  Pallas kernels: 0 us -> 127 us
  waiting for transfers between devices: 136 us -> 11.1 us
  other arithmetic: 116 us -> 3.17 us
  local copies, waits for them, and re-layouts: 76.2 us -> 17.4 us
  matrix products: 45.8 us -> 2.35 us
  blocking collectives: 40 us -> 0 us
  between operations: 15.9 us -> 0.85 us
    pallas_call x0 -> x6, Pallas kernels: none -> 127 us  [the longest x1 60.4 us: reduce_grads(): pl.pallas_call(functools.partial(reduce_kernel, tuple(bits), tuple(orders...]
    unnamed x2 -> x0, waiting for transfers between devices: 116 us -> none
    convert_element_type x6 -> x0, other arithmetic: 49.2 us -> none  [the longest x1 43 us: local(): attn = attn.astype(jnp.bfloat16).transpose(0, 3, 1, 2).reshape(-1, width)]
    dot_general x9 -> x1, matrix products: 45.8 us -> 2.35 us  [local(): jnp.einsum('ho,oqk->hqk', rel_bias, hot, precision=lax.Precision.HIGHEST)]
    psum x1 -> x0, blocking collectives: 40 us -> none  [local(): total = lax.psum(jnp.sum(share * share), ('row', 'col'))]
    dot_general x3 -> x0, other arithmetic: 31.9 us -> none  [local(): jnp.einsum('rhdc,rhdc->rhc', query_t, key, preferred_element_type=jnp.flo...]
    unnamed x133 -> x18, local copies, waits for them, and re-layouts: 30.3 us -> 4.62 us
    convert_element_type x6 -> x0, local copies, waits for them, and re-layouts: 14.6 us -> none  [the longest x3 8.49 us: local(): joined = out_y.reshape(rows // 2, 2, cols // 2, 2, width).transpose(0, 2,...]
  transfers between devices with their start and end apart: 5 -> 4, of which waited for: 2 -> 1; matrix products, arithmetic and copies ran while one was open for 5% -> 7% of each run, Pallas kernels for 0% -> 6%
where the time goes in v2:
time: 173 us; the launch traced here: 172 us
  Pallas kernels  127 us (73%)
  local copies, waits for them, and re-layouts  17.4 us (10%)
  waiting for transfers between devices  11.1 us (6%)
  starting transfers between devices  10 us (6%)
  other arithmetic  3.17 us (2%)
  matrix products  2.35 us (1%)
    pallas_call x1, Pallas kernels, reduce_grads(): pl.pallas_call(functools.partial(reduce_kernel, tuple(bits), tuple(orders...  60.4 us
    pallas_call x1, Pallas kernels, local(): pl.pallas_call(functools.partial(attend_kernel, heads, head_dim), grid=(b...  29.2 us
    pallas_call x1, Pallas kernels, local(): pl.pallas_call(functools.partial(grad_kernel, sub), in_specs=[pl.BlockSpe...  15.6 us
    pallas_call x1, Pallas kernels, local(): pl.pallas_call(functools.partial(mlp_kernel, sub), grid=(4,), in_specs=[p...  12.1 us
    ppermute x2, waiting for transfers between devices, shifted(): lax.ppermute(tail, axis, [(i, (i + 1) % count) for i in range(ends)])  11.1 us
    ppermute x2, starting transfers between devices, shifted(): lax.ppermute(tail, axis, [(i, (i + 1) % count) for i in range(ends)])  7.45 us
    pallas_call x1, Pallas kernels, local(): pl.pallas_call(back_kernel, grid=(4,), in_specs=[pl.BlockSpec((merged_cou...  5.3 us
    pallas_call x1, Pallas kernels, local(): pl.pallas_call(query_kernel, grid=(4,), in_specs=[pl.BlockSpec((step, wid...  4.71 us
  transfers between devices with their start and end apart: 4, of which 1 were waited for; matrix products, arithmetic and copies ran while one was open for 7% of the time, Pallas kernels for 6%

profile of v2, /device:TPU:0, one launch (start us, length us, event | category | flops | bytes accessed | tf_op | source)
XLA Modules:
  0.0 172.2 jit_solution(13442274475104405345)
XLA Ops:
  0.7 2.0 %fusion.20 = (bf16[3,128,512]{2,1,0:T(8,128)(2,1)S(1)}, bf16[3,128,512]{2,1,0:T(8,128)(2,1)}) fusion(bf16[8,128,512]{2,1,0:T(8,128)(2,1)} %param.11), kind=kLoop, calls=%fused_computation.63 | loop fusion | bytes 1572864 | tf_op jit(solution)/shard_map/slice | solution.py:23
  2.7 1.3 collective-permute-start.1
  3.9 5.5 %collective-permute-start = (bf16[3,128,512]{2,1,0:T(8,128)(2,1)}, bf16[3,128,512]{2,1,0:T(8,128)(2,1)S(1)}, u32[]{:S(2)}, u32[]{:S(2)}) collective-permute-start(bf16[3,128,512]{2,1,0:T(8,128)(2,1)} %get-tuple-element.18), channel_id=1, source_target_pairs={{0,4},{4,8},{8,12},{12,16},{16,20},{20,24},{24,28},{1,5},{5,9},{9,... | collective-permute-start | bytes 1179656 | tf_op jit(solution)/shard_map/ppermute | solution.py:25
  10.2 0.9 reshape.301.cot_ref
  11.1 2.4 %fusion.3 = f32[16,64,224]{2,0,1:T(8,128)} fusion(s32[64,224]{1,0:T(8,128)S(1)} %fusion.5, pred[64,224]{1,0:T(8,128)(4,1)S(1)} %fusion.9, f32[16,49]{1,0:T(8,128)S(1)} %copy-done), kind=kOutput, calls=%fused_computation.5 | convolution fusion | flops 135804928 | bytes 992320 | tf_op jit(solution)/shard_map/ho,oqk->hqk/dot_general | solution.py:383
  14.2 11.1 %collective-permute-done = bf16[3,128,512]{2,1,0:T(8,128)(2,1)S(1)} collective-permute-done((bf16[3,128,512]{2,1,0:T(8,128)(2,1)}, bf16[3,128,512]{2,1,0:T(8,128)(2,1)S(1)}, u32[]{:S(2)}, u32[]{:S(2)}) %collective-permute-start) | collective-permute-done | bytes 393248 | tf_op jit(solution)/shard_map/ppermute | solution.py:25
  25.5 1.3 copy-done.4
  26.8 1.9 %collective-permute-start.2 = (bf16[14,4,512]{2,1,0:T(4,128)(2,1)S(1)}, bf16[14,4,512]{2,1,0:T(4,128)(2,1)S(1)}, u32[]{:S(2)}, u32[]{:S(2)}) collective-permute-start(bf16[14,4,512]{2,1,0:T(4,128)(2,1)S(1)} %get-tuple-element.15), channel_id=1, source_target_pairs={{0,1},{1,2},{2,3},{4,5},{5,6},{6,7},{8,9},{9,10},{10,11},{12,13},{... | collective-permute-start | bytes 172040 | tf_op jit(solution)/shard_map/ppermute | solution.py:25
  28.7 1.3 collective-permute-start.3
  30.0 5.3 %back.1.gn_ref = f32[256,2048]{1,0:T(8,128)} custom-call(bf16[256,1024]{1,0:T(8,128)(2,1)} %reshape.301.cot_ref, bf16[2048,1024]{1,0:T(8,128)(2,1)} %wm_ref.1, f32[1,2048]{1,0:T(1,128)} %bitcast.22), custom_call_target="tpu_custom_call" | custom-call | flops 1073741824 | bytes 4718592 | tf_op jit(solution)/shard_map/back/pallas_call | solution.py:358
  35.3 1.2 reshape.297
  36.5 2.9 %copy.15 = f32[16,64,224]{2,1,0:T(8,128)} copy(f32[16,64,224]{2,0,1:T(8,128)} %fusion.3) | data formatting | bytes 1835008 | tf_op jit(solution)/shard_map/jit(_where)/select_n | solution.py:385
  39.5 1.1 slice.19.w_ref
  41.2 1.1 reshape.298.x_ref
  42.3 4.7 %query.1.q_ref = bf16[1024,512]{1,0:T(8,128)(2,1)} custom-call(bf16[1024,512]{1,0:T(8,128)(2,1)} %reshape.298.x_ref, f32[1,512]{1,0:T(1,128)} %bitcast.24, bf16[512,1536]{1,0:T(8,128)(2,1)} %w_ref.2), custom_call_target="tpu_custom_call" | custom-call | flops 536870912 | bytes 2097152 | tf_op jit(solution)/shard_map/query/pallas_call | solution.py:345
  47.0 2.2 %pad_maximum_fusion.x_ref = bf16[14,136,512]{2,1,0:T(8,128)(2,1)} fusion(bf16[14,4,512]{2,1,0:T(4,128)(2,1)S(1)} %collective-permute-done.3, bf16[14,128,512]{2,1,0:T(8,128)(2,1)S(1)} %copy-done.5, bf16[14,4,512]{2,1,0:T(4,128)(2,1)S(1)} %collective-permute-done.2), kind=kLoop, calls=%fused_computation.2 | loop fusion | flops 5849088 | bytes 3899392 | tf_op jit(solution)/shard_map/concatenate | solution.py:397
  49.2 29.2 %attend.1.a_ref = bf16[1024,512]{1,0:T(8,128)(2,1)} custom-call(bf16[14,136,512]{2,1,0:T(8,128)(2,1)} %pad_maximum_fusion.x_ref, f32[1,512]{1,0:T(1,128)} %bitcast.25, bf16[512,1024]{1,0:T(8,128)(2,1)} %slice.19.w_ref, bf16[1024,512]{1,0:T(8,128)(2,1)} %query.1.q_ref, f32[2,512,224]{2,1,0:T(8,128)} %bitcast.21, f32[16,1,224]{2,1,0:T(1,128)} %and_select_fusion.edge_ref), custom_call_target="tpu_custom_call" | custom-call | flops 4294967296 | bytes 2867200 | tf_op jit(solution)/shard_map/attend/pallas_call | solution.py:401
  78.4 12.1 %mlp.1 = (bf16[1024,2048]{1,0:T(8,128)(2,1)}, bf16[256,2048]{1,0:T(8,128)(2,1)}) custom-call(bf16[1024,512]{1,0:T(8,128)(2,1)} %attend.1.a_ref, bf16[1024,512]{1,0:T(8,128)(2,1)} %reshape.298.x_ref, f32[1,512]{1,0:T(1,128)} %bitcast.26, bf16[512,512]{1,0:T(8,128)(2,1)} %wp_ref.1, bf16[512,2048]{1,0:T(8,128)(2,1)} %wu_ref.1, bf16[2048,512]{1,0:T(8,128)(2,1)} %wd_ref.1), custom_call_target="tpu_custom_call" | custom-call | flops 4294967296 | bytes 4194304 | tf_op jit(solution)/shard_map/mlp/pallas_call | solution.py:420
  90.5 15.6 %grads.1 = (bf16[256,1024]{1,0:T(8,128)(2,1)}, bf16[3,2048,512]{2,1,0:T(8,128)(2,1)}) custom-call(bf16[256,2048]{1,0:T(8,128)(2,1)} %get-tuple-element.9.z_ref, bf16[1024,2048]{1,0:T(8,128)(2,1)} %get-tuple-element.10.hid_ref, f32[256,2048]{1,0:T(8,128)} %back.1.gn_ref, bf16[256,1024]{1,0:T(8,128)(2,1)} %reshape.301.cot_ref, f32[1,2048]{1,0:T(1,128)} %bitcast.23, ...), custom_call_target="tpu_custom_call" | custom-call | flops 2147483648 | bytes 4194304 | tf_op jit(solution)/shard_map/grads/pallas_call | solution.py:444
  106.1 1.2 reshape.302
  107.6 0.9 reshape.303
  108.5 60.4 %reduce.1 = (f32[64,1024]{1,0:T(8,128)}, f32[64,512]{1,0:T(8,128)}) custom-call(bf16[3,2,2,2,2,2,64,512]{7,6,5,4,3,2,1,0:T(8,128)(2,1)} %bitcast.17), custom_call_target="tpu_custom_call" | custom-call | tf_op jit(solution)/shard_map/reduce/pallas_call | solution.py:277
  168.9 1.7 copy.26
  170.6 1.6 copy.27
  (32 shorter events, 2.4 us)
Async XLA Ops:
  0.6 10.5 %copy-start = (f32[16,49]{1,0:T(8,128)S(1)}, f32[16,49]{1,0:T(8,128)}, u32[]{:S(2)}) copy-start(f32[16,49]{1,0:T(8,128)} %param.14) | copy-start | bytes 9412
  0.6 9.1 %copy-start.6 = (bf16[4,64,1024]{2,1,0:T(8,128)(2,1)S(1)}, bf16[4,64,1024]{2,1,0:T(8,128)(2,1)}, u32[]{:S(2)}) copy-start(bf16[4,64,1024]{2,1,0:T(8,128)(2,1)} %param.21) | copy-start | bytes 1572868
  2.7 22.8 %collective-permute-start.1 = (bf16[3,128,512]{2,1,0:T(8,128)(2,1)S(1)}, bf16[3,128,512]{2,1,0:T(8,128)(2,1)S(1)}, u32[]{:S(2)}, u32[]{:S(2)}) collective-permute-start(bf16[3,128,512]{2,1,0:T(8,128)(2,1)S(1)} %get-tuple-element.17), channel_id=1, source_target_pairs={{4,0},{8,4},{12,8},{16,12},{20,16},{24,20},{28,24},{5,1},{9,5},{13... | collective-permute-start | bytes 1179656 | tf_op jit(solution)/shard_map/ppermute | solution.py:26
  3.9 21.4 %collective-permute-start = (bf16[3,128,512]{2,1,0:T(8,128)(2,1)}, bf16[3,128,512]{2,1,0:T(8,128)(2,1)S(1)}, u32[]{:S(2)}, u32[]{:S(2)}) collective-permute-start(bf16[3,128,512]{2,1,0:T(8,128)(2,1)} %get-tuple-element.18), channel_id=1, source_target_pairs={{0,4},{4,8},{8,12},{12,16},{16,20},{20,24},{24,28},{1,5},{5,9},{9,... | collective-permute-start | bytes 1179656 | tf_op jit(solution)/shard_map/ppermute | solution.py:25
  10.0 15.4 %copy-start.1 = (bf16[8,128,512]{2,1,0:T(8,128)(2,1)S(1)}, bf16[8,128,512]{2,1,0:T(8,128)(2,1)}, u32[]{:S(2)}) copy-start(bf16[8,128,512]{2,1,0:T(8,128)(2,1)} %param.11) | copy-start | bytes 3145732
  25.5 1.3 copy-start.4
  26.8 20.2 %collective-permute-start.2 = (bf16[14,4,512]{2,1,0:T(4,128)(2,1)S(1)}, bf16[14,4,512]{2,1,0:T(4,128)(2,1)S(1)}, u32[]{:S(2)}, u32[]{:S(2)}) collective-permute-start(bf16[14,4,512]{2,1,0:T(4,128)(2,1)S(1)} %get-tuple-element.15), channel_id=1, source_target_pairs={{0,1},{1,2},{2,3},{4,5},{5,6},{6,7},{8,9},{9,10},{10,11},{12,13},{... | collective-permute-start | bytes 172040 | tf_op jit(solution)/shard_map/ppermute | solution.py:25
  28.7 18.3 %collective-permute-start.3 = (bf16[14,4,512]{2,1,0:T(4,128)(2,1)S(1)}, bf16[14,4,512]{2,1,0:T(4,128)(2,1)S(1)}, u32[]{:S(2)}, u32[]{:S(2)}) collective-permute-start(bf16[14,4,512]{2,1,0:T(4,128)(2,1)S(1)} %get-tuple-element.16), channel_id=1, source_target_pairs={{1,0},{2,1},{3,2},{5,4},{6,5},{7,6},{9,8},{10,9},{11,10},{13,12},{... | collective-permute-start | bytes 172040 | tf_op jit(solution)/shard_map/ppermute | solution.py:26
  35.3 4.1 %copy-start.2 = (bf16[512,1536]{1,0:T(8,128)(2,1)S(1)}, bf16[512,1536]{1,0:T(8,128)(2,1)}, u32[]{:S(2)}) copy-start(bf16[512,1536]{1,0:T(8,128)(2,1)} %w_ref.2) | copy-start | bytes 4718596
  36.5 4.0 %copy-start.3 = (bf16[4,2,16,4,2,512]{5,4,3,2,1,0:T(2,128)(2,1)S(1)}, bf16[4,2,16,4,2,512]{5,4,3,2,1,0:T(2,128)(2,1)}, u32[]{:S(2)}) copy-start(bf16[4,2,16,4,2,512]{5,4,3,2,1,0:T(2,128)(2,1)} %reshape.297) | copy-start | bytes 3145732
  42.3 4.7 %copy-start.5 = (bf16[14,128,512]{2,1,0:T(8,128)(2,1)S(1)}, bf16[14,128,512]{2,1,0:T(8,128)(2,1)}, u32[]{:S(2)}) copy-start(bf16[14,128,512]{2,1,0:T(8,128)(2,1)} %copy-done.4) | copy-start | bytes 5505028
